TPU v7x, 128 devices: a whole 4x4x4 slice. The times are simulated.
128 devices in a mesh: group: 4 (over x), cluster: 32 (over z, y, core).
Axes of the slice: x: 4, y: 4, z: 4, core: 2. Of those that a mesh axis runs over, the one named last changes fastest.
Arguments:
- charges: float32 [1048576, 128], P(('group', 'cluster')), may hold values from -6 to 6
- leaf_size: int32 [4096], P(('group', 'cluster')), may hold values from 1 to 256, 786432 in all
- leaf_basis: float32 [4096, 64, 256], P(('group', 'cluster')), may hold values from -0.375 to 0.375
- leaf_transfer: float32 [4096, 64, 64], P(('group', 'cluster')), may hold values from -0.375 to 0.375
- mid_transfer: float32 [1024, 64, 64], P(('group', 'cluster')), may hold values from -0.25 to 0.25
- leaf_parent: int32 [4096], P(('group', 'cluster')), may hold values from 0 to 7, as said below
- send_leaf: int32 [32768], P(('group', 'cluster')), may hold values from 0 to 32, as said below
- pair_leaf: int32 [4096, 12], P(('group', 'cluster')), may hold values from 0 to 256, as said below
- leaf_coupling: float32 [4096, 64, 768], P(('group', 'cluster')), may hold values from -0.21875 to 0.21875
- send_mid: int32 [32768], P(('group', 'cluster')), may hold values from 0 to 8, as said below
- pair_mid: int32 [1024, 32], P(('group', 'cluster')), may hold values from 0 to 256, as said below
- mid_coupling: float32 [1024, 64, 2048], P(('group', 'cluster')), may hold values from -0.125 to 0.125
- top_pairs: int32 [128, 4], P('group'), may hold values from 0 to 128, as said below
- top_coupling: float32 [128, 64, 256], P('group'), may hold values from -0.375 to 0.375
Outputs:
- far_field: float32 [1048576, 128], P(('group', 'cluster'))
Inputs may be any that keep to these rules, and one draw needn't show every extreme that they name: `send_leaf`: entry (d * 128 + r) * 2 + j is the leaf, local to device d, whose block d puts in slot j for device r, or 32 for an empty slot; the leaves in one sender's slots to one receiver are distinct; some receiver has every slot from every sender filled. `pair_leaf`: row t names leaf t's admissible partners as positions 2 * d + j among the slots its owner receives, filled slots only and distinct within a row, or 256 for no partner; every filled slot is named by some row of its receiver. `send_mid`: as send_leaf, for level-one clusters: local indices below 8, 8 for an empty slot; some receiver has every slot from every sender filled. `pair_mid`: as pair_leaf, for level-one clusters; every filled slot is named by some row of its receiver. `leaf_parent`: every level-one cluster of a device is the parent of at least one of its leaves. `top_pairs`: row o names coarse clusters other than o, distinct within a row, at least one a row, or 128 for no partner.
All inputs are finite; a program needn't handle non-finite values. No bound on the sum of `leaf_size` on one device may be relied on, other than what follows from the above.
Results may differ from a plain program's by a relative error of at most 0.000062.
Values sent between devices are 32-bit elements; how exact they have to be, the bound alone decides.
A program may use at most 128 MiB of HBM per device.

v0:
```python
import jax
import jax.numpy as jnp
from jax import lax
from jax.sharding import PartitionSpec as P

exact_mode = lax.Precision.HIGHEST


def couple(coupling, coef, index):
    stacked = jnp.take(coef, index, axis=0, mode="fill", fill_value=0.0)
    stacked = stacked.reshape(index.shape[0], index.shape[1] * coef.shape[1], coef.shape[2])
    return jnp.einsum("nkq,nqp->nkp", coupling, stacked, precision=exact_mode)


def body(
    charges,
    leaf_size,
    leaf_basis,
    leaf_transfer,
    mid_transfer,
    leaf_parent,
    send_leaf,
    pair_leaf,
    leaf_coupling,
    send_mid,
    pair_mid,
    mid_coupling,
    top_pairs,
    top_coupling,
):
    leaf_count, coef_rank, leaf_points = leaf_basis.shape
    port_count = charges.shape[1]
    mid_count = mid_transfer.shape[0]
    owners = send_leaf.shape[0] // 2
    slots = 2
    point_mask = (jnp.arange(leaf_points, dtype=jnp.int32)[None, :] < leaf_size[:, None]).astype(
        jnp.float32
    )
    blocks = charges.reshape(leaf_count, leaf_points, port_count) * point_mask[:, :, None]
    coef_leaf = jnp.einsum("lkm,lmp->lkp", leaf_basis, blocks, precision=exact_mode)
    moved_up = jnp.einsum("ljk,lkp->ljp", leaf_transfer, coef_leaf, precision=exact_mode)
    parent_map = (leaf_parent[None, :] == jnp.arange(mid_count, dtype=jnp.int32)[:, None]).astype(
        jnp.float32
    )
    coef_mid = jnp.einsum("ml,ljp->mjp", parent_map, moved_up, precision=exact_mode)
    coef_top = jnp.einsum("mjk,mkp->jp", mid_transfer, coef_mid, precision=exact_mode)
    outgoing_leaf = jnp.take(coef_leaf, send_leaf, axis=0, mode="fill", fill_value=0.0)
    outgoing_mid = jnp.take(coef_mid, send_mid, axis=0, mode="fill", fill_value=0.0)
    outgoing = jnp.concatenate(
        [
            outgoing_leaf.reshape(owners, slots, coef_rank, port_count),
            outgoing_mid.reshape(owners, slots, coef_rank, port_count),
        ],
        axis=1,
    ).reshape(owners * 2 * slots, coef_rank, port_count)
    arrived = lax.all_to_all(
        outgoing, ("group", "cluster"), split_axis=0, concat_axis=0, tiled=True
    )
    listed = top_pairs.shape[1]
    position = lax.axis_index("cluster")
    wanted = lax.dynamic_slice_in_dim(top_pairs, position, 1, 0)[0]
    own_coupling = lax.dynamic_slice_in_dim(top_coupling, position, 1, 0)[0]
    shard_rows = lax.all_gather(coef_top[None], ("group", "cluster"), axis=0, tiled=True)
    inside = (wanted >= 0) & (wanted < shard_rows.shape[0])
    taken_rows = jnp.take(shard_rows, jnp.clip(wanted, 0, shard_rows.shape[0] - 1), axis=0)
    picked = jnp.where(
        inside[:, None, None], taken_rows, jnp.zeros((listed, coef_rank, port_count), jnp.float32)
    )
    near_top = jnp.einsum(
        "kq,qp->kp",
        own_coupling,
        picked.reshape(listed * coef_rank, port_count),
        precision=exact_mode,
    )
    total_rows = owners * 2 * slots
    live_leaf = pair_leaf < owners * slots
    leaf_rows = jnp.where(live_leaf, pair_leaf + pair_leaf // slots * slots, total_rows)
    near_leaf = couple(leaf_coupling, arrived, leaf_rows)
    live_mid = pair_mid < owners * slots
    mid_rows = jnp.where(live_mid, pair_mid + (pair_mid // slots + 1) * slots, total_rows)
    near_mid = couple(mid_coupling, arrived, mid_rows)
    down_mid = near_mid + jnp.einsum("mjk,jp->mkp", mid_transfer, near_top, precision=exact_mode)
    from_parent = jnp.einsum("ml,mkp->lkp", parent_map, down_mid, precision=exact_mode)
    down_leaf = near_leaf + jnp.einsum(
        "ljk,ljp->lkp", leaf_transfer, from_parent, precision=exact_mode
    )
    far_field = (
        jnp.einsum("lkm,lkp->lmp", leaf_basis, down_leaf, precision=exact_mode)
        * point_mask[:, :, None]
    )
    return far_field.reshape(leaf_count * leaf_points, port_count)


def solution(mesh):
    in_specs = (
        P(("group", "cluster"), None),
        P(("group", "cluster")),
        P(("group", "cluster"), None, None),
        P(("group", "cluster"), None, None),
        P(("group", "cluster"), None, None),
        P(("group", "cluster")),
        P(("group", "cluster")),
        P(("group", "cluster"), None),
        P(("group", "cluster"), None, None),
        P(("group", "cluster")),
        P(("group", "cluster"), None),
        P(("group", "cluster"), None, None),
        P("group", None),
        P("group", None, None),
    )
    out_specs = P(("group", "cluster"), None)
    return jax.shard_map(body, mesh=mesh, in_specs=in_specs, out_specs=out_specs, check_vma=False)
```

profile of v0, /device:TPU:1, one launch (start us, length us, event | category | flops | bytes accessed | tf_op | source)
XLA Modules:
  0.0 382.9 jit_solution(8333064227275518542)
XLA Ops:
  6.5 0.8 compare_select_fusion.3
  7.4 0.7 compare_and_fusion.4
  8.1 0.7 compare_select_fusion.2
  8.7 0.7 compare_and_fusion.3
  9.4 0.7 fusion.11
  10.2 5.1 %fusion = f32[32,128,64]{1,2,0:T(8,128)S(1)} fusion(f32[32,64,256]{2,1,0:T(8,128)S(1)} %copy-done, f32[32,256,128]{2,1,0:T(8,128)} %bitcast.64, f32[32,256]{1,0:T(8,128)S(1)} %fusion.11), kind=kOutput, calls=%fused_computation.11 | convolution fusion | flops 806354944 | bytes 7372800 | tf_op jit(solution)/shard_map/lkm,lmp->lkp/dot_general | solution.py:40
  15.3 2.3 fusion.31
  17.6 1.0 fusion.4
  18.6 0.0 copy-start.4
  18.7 0.7 copy-done.4
  19.3 0.1 copy.19
  19.4 0.2 broadcast_in_dim.101
  19.6 0.2 broadcast_in_dim.105
  19.8 4.4 %gather_fusion.1 = f32[256,64,128]{2,1,0:T(8,128)} fusion(f32[8,64,128]{2,1,0:T(8,128)S(1)} %copy.19, s32[1024]{0:T(1024)S(1)} %pad_clamp_fusion.3), kind=kCustom, calls=%fused_computation.1 | custom fusion | bytes 16778240 | tf_op jit(solution)/shard_map/jit(_take)/gather | solution.py:48
  24.1 4.4 %gather_fusion = f32[256,64,128]{2,1,0:T(8,128)} fusion(f32[32,64,128]{2,1,0:T(8,128)S(1)} %bitcast.58, s32[1024]{0:T(1024)S(1)} %pad_clamp_fusion.4), kind=kCustom, calls=%fused_computation | custom fusion | bytes 16778240 | tf_op jit(solution)/shard_map/jit(_take)/gather | solution.py:47
  28.5 6.5 %broadcast_select_fusion = (f32[128,2,64,128]{3,2,1,0:T(8,128)S(1)}, f32[128,2,64,128]{3,2,1,0:T(8,128)S(1)}) fusion(f32[128,2,64,128]{3,2,1,0:T(8,128)} %bitcast.61, pred[128,2]{1,0:T(8,128)(4,1)S(1)} %broadcast_in_dim.105, f32[128,2,64,128]{3,2,1,0:T(8,128)} %bitcast.62, pred[128,2]{1,0:T(8,128)(4,1)S(1)} %broadcast_in_dim.101), kind=kLoop, calls=%fused_computation.9 | loop fusion | flops 4194304 | bytes 33554944 | tf_op jit(solution)/shard_map/jit(_take)/select_n | solution.py:48
  35.0 6.1 %pad_maximum_fusion = f32[128,4,64,128]{3,2,1,0:T(8,128)} fusion(f32[128,2,64,128]{3,2,1,0:T(8,128)S(1)} %get-tuple-element.9, f32[128,2,64,128]{3,2,1,0:T(8,128)S(1)} %get-tuple-element.10), kind=kLoop, calls=%fused_computation.5 | loop fusion | flops 4194304 | bytes 33554432 | tf_op jit(solution)/shard_map/concatenate | solution.py:49
  41.1 12.0 %all-to-all-start = ((f32[512,64,128]{2,1,0:T(8,128)}), f32[512,64,128]{2,1,0:T(8,128)}, u32[]{:S(2)}, u32[]{:S(2)}) async-start(f32[512,64,128]{2,1,0:T(8,128)} %bitcast.59), calls=%async_computation | async-start | bytes 33554432 | tf_op jit(solution)/shard_map/all_to_all | solution.py:56
  53.1 0.0 all-gather.3.cloned.1.call-start
  53.1 0.1 copy.25
  53.3 1.2 convolution_bitcast_fusion.3
  54.5 0.0 all-gather.3.cloned.1.call-update
  54.6 0.1 reshape.198
  54.7 0.1 broadcast_in_dim.111
  54.8 0.1 broadcast_in_dim.112
  54.9 0.1 copy.20
  55.0 0.1 reshape.190
  55.1 0.1 copy.18
  55.2 0.1 broadcast_in_dim.98
  55.4 0.1 broadcast_in_dim.99
  55.5 0.2 clamp_reduce_fusion
  55.7 0.2 and_reduce_fusion
  55.9 238.2 %all-gather.3.cloned.1.call-done = f32[8192,128]{1,0:T(8,128)} async-done(((f32[64,128]{1,0:T(8,128)}), f32[8192,128]{1,0:T(8,128)}) %all-gather.3.cloned.1.call-update) | async-done | bytes 4194320 | tf_op jit(solution)/shard_map/all_gather | solution.py:63
  294.1 2.7 gather_fusion.4
  296.9 0.1 select_select_fusion
  297.0 1.1 convolution_bitcast_fusion.2
  298.1 1.4 convolution_bitcast_fusion.1
  299.5 10.1 %gather_fusion.3 = f32[256,64,128]{2,1,0:T(8,128)} fusion(f32[512,64,128]{2,1,0:T(8,128)} %all-to-all-done, s32[1024]{0:T(1024)S(1)} %pad_clamp_fusion.1), kind=kCustom, calls=%fused_computation.3 | custom fusion | bytes 16778240 | tf_op jit(solution)/shard_map/jit(_take)/gather | solution.py:10
  309.6 7.5 %bitcast_select_fusion.1 = f32[8,2048,128]{2,1,0:T(8,128)S(1)} fusion(pred[8,2048]{1,0:T(8,128)(4,1)S(1)} %broadcast_in_dim.112, f32[8,2048,128]{2,1,0:T(8,128)} %bitcast.63), kind=kLoop, calls=%fused_computation.7 | loop fusion | flops 2097152 | bytes 16793600 | tf_op jit(solution)/shard_map/jit(_take)/select_n | solution.py:10
  317.1 14.3 %fusion.3 = f32[8,64,128]{1,2,0:T(8,128)} fusion(f32[8,64,128]{1,2,0:T(8,128)S(1)} %copy-done.6, f32[8,2048,128]{2,1,0:T(8,128)S(1)} %bitcast_select_fusion.1, f32[8,64,2048]{2,1,0:T(8,128)S(1)} %copy-done.3), kind=kOutput, calls=%fused_computation.16 | convolution fusion | flops 1610678272 | bytes 13107200 | tf_op jit(solution)/shard_map/nkq,nqp->nkp/dot_general | solution.py:12
  331.4 1.2 copy.26
  332.6 0.6 fusion.23
  333.3 3.3 fusion.6
  336.6 11.7 %gather_fusion.2 = f32[384,64,128]{2,1,0:T(8,128)} fusion(f32[512,64,128]{2,1,0:T(8,128)} %all-to-all-done, s32[1024]{0:T(1024)S(1)} %pad_clamp_fusion.2), kind=kCustom, calls=%fused_computation.2 | custom fusion | bytes 25167360 | tf_op jit(solution)/shard_map/jit(_take)/gather | solution.py:10
  348.2 6.1 %bitcast_select_fusion = f32[32,768,128]{2,1,0:T(8,128)S(1)} fusion(pred[32,768]{1,0:T(8,128)(4,1)S(1)} %broadcast_in_dim.99, f32[32,768,128]{2,1,0:T(8,128)} %bitcast.60), kind=kLoop, calls=%fused_computation.6 | loop fusion | flops 3145728 | bytes 25190400 | tf_op jit(solution)/shard_map/jit(_take)/select_n | solution.py:10
  354.4 10.9 %convolution_add_fusion = f32[32,128,64]{1,2,0:T(8,128)S(1)} fusion(f32[32,128,64]{1,2,0:T(8,128)S(1)} %copy-done.2, f32[32,768,128]{2,1,0:T(8,128)S(1)} %bitcast_select_fusion, f32[32,64,768]{2,1,0:T(8,128)} %param.22), kind=kOutput, calls=%fused_computation.14 | convolution fusion | flops 2416181248 | bytes 20971520 | tf_op jit(solution)/shard_map/nkq,nqp->nkp/dot_general | solution.py:12
  365.3 5.2 %multiply_bitcast_fusion = f32[32,256,128]{1,2,0:T(8,128)} fusion(f32[32,128,64]{1,2,0:T(8,128)S(1)} %convolution_add_fusion, f32[32,64,256]{2,1,0:T(8,128)S(1)} %copy-done, f32[32,256]{1,0:T(8,128)S(1)} %fusion.11), kind=kOutput, calls=%fused_computation.8 | convolution fusion | flops 806354944 | bytes 7372800 | tf_op jit(solution)/shard_map/lkm,lkp->lmp/dot_general | solution.py:88
  370.5 5.6 %copy.22 = f32[32,256,128]{2,1,0:T(8,128)} copy(f32[32,256,128]{1,2,0:T(8,128)} %multiply_bitcast_fusion) | data formatting | bytes 8388608 | tf_op jit(solution)/shard_map/mul | solution.py:88
  (32 shorter events, 0.1 us)
Async XLA Ops:
  6.5 3.6 copy-start
  6.5 11.1 %copy-start.11 = (s32[32]{0:T(128)S(1)}, s32[32]{0:T(128)}, u32[]{:S(2)}) copy-start(s32[32]{0:T(128)} %param.19) | copy-start | bytes 388
  18.6 0.7 copy-start.4
  41.1 12.0 %copy-start.7 = (f32[8,64,64]{2,1,0:T(8,128)S(1)}, f32[8,64,64]{2,1,0:T(8,128)}, u32[]{:S(2)}) copy-start(f32[8,64,64]{2,1,0:T(8,128)} %param.18) | copy-start | bytes 393220
  41.1 12.2 %copy-start.5 = (f32[8,64,128]{2,0,1:T(8,128)S(1)}, f32[8,64,128]{2,0,1:T(8,128)}, u32[]{:S(2)}) copy-start(f32[8,64,128]{2,0,1:T(8,128)} %copy-done.4) | copy-start | bytes 786436
  41.1 13.4 %copy-start.10 = (s32[8,32]{1,0:T(8,128)S(1)}, s32[8,32]{1,0:T(8,128)}, u32[]{:S(2)}) copy-start(s32[8,32]{1,0:T(8,128)} %param.24) | copy-start | bytes 3076
  41.1 13.8 %copy-start.9 = (s32[32,12]{0,1:T(8,128)S(1)}, s32[32,12]{0,1:T(8,128)}, u32[]{:S(2)}) copy-start(s32[32,12]{0,1:T(8,128)} %param.21) | copy-start | bytes 4612
  41.1 14.4 %copy-start.8 = (s32[32,4]{0,1:T(4,128)S(1)}, s32[32,4]{0,1:T(4,128)}, u32[]{:S(2)}) copy-start(s32[32,4]{0,1:T(4,128)} %param.26) | copy-start | bytes 1540
  41.1 258.4 %all-to-all-start = ((f32[512,64,128]{2,1,0:T(8,128)}), f32[512,64,128]{2,1,0:T(8,128)}, u32[]{:S(2)}, u32[]{:S(2)}) async-start(f32[512,64,128]{2,1,0:T(8,128)} %bitcast.59), calls=%async_computation | async-start | bytes 33554432 | tf_op jit(solution)/shard_map/all_to_all | solution.py:56
  53.1 241.1 %all-gather.3.cloned.1.call-start = ((), (), s32[]{:S(2)}) async-start(), calls=%async_computation.1 | async-start | bytes 4227072 | tf_op jit(solution)/shard_map/all_gather | solution.py:63
  309.6 7.5 %copy-start.3 = (f32[8,64,2048]{2,1,0:T(8,128)S(1)}, f32[8,64,2048]{2,1,0:T(8,128)}, u32[]{:S(2)}) copy-start(f32[8,64,2048]{2,1,0:T(8,128)} %param.25) | copy-start | bytes 12582916
  309.6 7.5 %copy-start.6 = (f32[8,64,128]{1,2,0:T(8,128)S(1)}, f32[8,64,128]{1,2,0:T(8,128)}, u32[]{:S(2)}) copy-start(f32[8,64,128]{1,2,0:T(8,128)} %convolution_bitcast_fusion.1) | copy-start | bytes 786436
  317.1 16.2 %copy-start.1 = (f32[32,64,64]{2,1,0:T(8,128)S(1)}, f32[32,64,64]{2,1,0:T(8,128)}, u32[]{:S(2)}) copy-start(f32[32,64,64]{2,1,0:T(8,128)} %param.17) | copy-start | bytes 1572868
  348.2 6.1 %copy-start.2 = (f32[32,128,64]{1,2,0:T(8,128)S(1)}, f32[32,128,64]{1,2,0:T(8,128)}, u32[]{:S(2)}) copy-start(f32[32,128,64]{1,2,0:T(8,128)} %fusion.6) | copy-start | bytes 3145732
Sparse Core Ops, SparseCore 0:
  57.1 237.0 all-gather.2
where the time goes:
time: 384 us; the launch traced here: 383 us
  waiting for transfers between devices  238 us (62%)
  matrix products  46.5 us (12%)
  local copies, waits for them, and re-layouts  42.1 us (11%)
  other arithmetic  30.3 us (8%)
  between operations  13.7 us (4%)
  starting transfers between devices  12 us (3%)
    all_gather x1, waiting for transfers between devices, body(): lax.all_gather(coef_top[None], ('group', 'cluster'), axis=0, tiled=True)  238 us
    dot_general x2, matrix products, couple(): return jnp.einsum('nkq,nqp->nkp', coupling, stacked, precision=exact_mode)  25.2 us
    gather x2, local copies, waits for them, and re-layouts, couple(): stacked = jnp.take(coef, index, axis=0, mode='fill', fill_value=0.0)  21.8 us
    select_n x2, other arithmetic, couple(): stacked = jnp.take(coef, index, axis=0, mode='fill', fill_value=0.0)  13.6 us
    all_to_all x1, starting transfers between devices, body(): lax.all_to_all(outgoing, ('group', 'cluster'), split_axis=0, concat_axis=...  12 us
  transfers between devices with their start and end apart: 2, of which 1 were waited for; matrix products, arithmetic and copies ran while one was open for 2% of the time, Pallas kernels for 0%

commit v1 on v0

--- a/solution.py
+++ b/solution.py
@@ -60,7 +60,11 @@
     position = lax.axis_index("cluster")
     wanted = lax.dynamic_slice_in_dim(top_pairs, position, 1, 0)[0]
     own_coupling = lax.dynamic_slice_in_dim(top_coupling, position, 1, 0)[0]
-    shard_rows = lax.all_gather(coef_top[None], ("group", "cluster"), axis=0, tiled=True)
+    block = coef_top[None]
+    peers = lax.axis_size(("group", "cluster"))
+    shards = jnp.stack([block for _ in range(peers)])
+    shards = lax.all_to_all(shards, ("group", "cluster"), split_axis=0, concat_axis=0)
+    shard_rows = jnp.concatenate(shards, axis=0)
     inside = (wanted >= 0) & (wanted < shard_rows.shape[0])
     taken_rows = jnp.take(shard_rows, jnp.clip(wanted, 0, shard_rows.shape[0] - 1), axis=0)
     picked = jnp.where(

time: 384 us -> 403 us (1.049)
  the two profiles are of different devices: /device:TPU:1 before, /device:TPU:98 now
where the time goes in v1:
time: 403 us; the launch traced here: 402 us
  waiting for transfers between devices  262 us (65%)
  local copies, waits for them, and re-layouts  46.6 us (12%)
  matrix products  45.9 us (11%)
  other arithmetic  27.6 us (7%)
  starting transfers between devices  19.3 us (5%)
    all_to_all x1, waiting for transfers between devices, body(): lax.all_to_all(outgoing, ('group', 'cluster'), split_axis=0, concat_axis=...  235 us
    all_to_all x1, waiting for transfers between devices, body(): lax.all_to_all(shards, ('group', 'cluster'), split_axis=0, concat_axis=0)  27 us
    dot_general x2, matrix products, couple(): return jnp.einsum('nkq,nqp->nkp', coupling, stacked, precision=exact_mode)  25.2 us
    gather x2, local copies, waits for them, and re-layouts, couple(): stacked = jnp.take(coef, index, axis=0, mode='fill', fill_value=0.0)  21.8 us
    select_n x2, other arithmetic, couple(): stacked = jnp.take(coef, index, axis=0, mode='fill', fill_value=0.0)  13.6 us
    all_to_all x1, starting transfers between devices, body(): lax.all_to_all(shards, ('group', 'cluster'), split_axis=0, concat_axis=0)  10.3 us
    all_to_all x1, starting transfers between devices, body(): lax.all_to_all(outgoing, ('group', 'cluster'), split_axis=0, concat_axis=...  9.03 us
  transfers between devices with their start and end apart: 2, of which 2 were waited for; matrix products, arithmetic and copies ran while one was open for 7% of the time, Pallas kernels for 0%

profile of v1, /device:TPU:98, one launch (start us, length us, event | category | flops | bytes accessed | tf_op | source)
XLA Modules:
  0.0 402.0 jit_solution(11334456449263422739)
XLA Ops:
  0.0 0.9 fusion.11
  0.9 1.1 copy.25
  2.0 5.1 %fusion = f32[32,128,64]{1,2,0:T(8,128)S(1)} fusion(f32[32,64,256]{2,1,0:T(8,128)S(1)} %copy-done, f32[32,256,128]{2,1,0:T(8,128)} %bitcast.64, f32[32,256]{1,0:T(8,128)S(1)} %fusion.11), kind=kOutput, calls=%fused_computation.11 | convolution fusion | flops 806354944 | bytes 7372800 | tf_op jit(solution)/shard_map/lkm,lmp->lkp/dot_general | solution.py:40
  7.1 0.0 copy-start.11
  7.1 0.0 copy-start.12
  7.1 2.3 fusion.31
  9.5 0.0 copy-done.10
  9.5 1.0 fusion.4
  10.5 0.7 copy-done.4
  11.2 0.6 convolution_bitcast_fusion.3
  11.8 2.5 stack.3
  14.4 10.3 %all-to-all-start.1 = ((f32[128,1,64,128]{3,2,1,0:T(8,128)}), f32[128,1,64,128]{3,2,1,0:T(8,128)}, u32[]{:S(2)}, u32[]{:S(2)}) async-start(f32[128,1,64,128]{3,2,1,0:T(8,128)} %stack.3), calls=%async_computation.1 | async-start | bytes 8388608 | tf_op jit(solution)/shard_map/all_to_all | solution.py:66
  24.7 1.0 copy.19
  25.7 0.2 broadcast_in_dim.102
  25.9 0.2 broadcast_in_dim.98
  26.1 4.4 %gather_fusion.1 = f32[256,64,128]{2,1,0:T(8,128)} fusion(f32[8,64,128]{2,1,0:T(8,128)S(1)} %copy.19, s32[1024]{0:T(1024)S(1)} %pad_clamp_fusion.3), kind=kCustom, calls=%fused_computation.1 | custom fusion | bytes 16778240 | tf_op jit(solution)/shard_map/jit(_take)/gather | solution.py:48
  30.4 4.4 %gather_fusion = f32[256,64,128]{2,1,0:T(8,128)} fusion(f32[32,64,128]{2,1,0:T(8,128)S(1)} %bitcast.58, s32[1024]{0:T(1024)S(1)} %pad_clamp_fusion.4), kind=kCustom, calls=%fused_computation | custom fusion | bytes 16778240 | tf_op jit(solution)/shard_map/jit(_take)/gather | solution.py:47
  34.8 6.5 %broadcast_select_fusion = (f32[128,2,64,128]{3,2,1,0:T(8,128)S(1)}, f32[128,2,64,128]{3,2,1,0:T(8,128)S(1)}) fusion(f32[128,2,64,128]{3,2,1,0:T(8,128)} %bitcast.61, pred[128,2]{1,0:T(8,128)(4,1)S(1)} %broadcast_in_dim.102, f32[128,2,64,128]{3,2,1,0:T(8,128)} %bitcast.62, pred[128,2]{1,0:T(8,128)(4,1)S(1)} %broadcast_in_dim.98), kind=kLoop, calls=%fused_computation.9 | loop fusion | flops 4194304 | bytes 33554944 | tf_op jit(solution)/shard_map/jit(_take)/select_n | solution.py:48
  41.4 6.1 %pad_maximum_fusion = f32[128,4,64,128]{3,2,1,0:T(8,128)} fusion(f32[128,2,64,128]{3,2,1,0:T(8,128)S(1)} %get-tuple-element.9, f32[128,2,64,128]{3,2,1,0:T(8,128)S(1)} %get-tuple-element.10), kind=kLoop, calls=%fused_computation.5 | loop fusion | flops 4194304 | bytes 33554432 | tf_op jit(solution)/shard_map/concatenate | solution.py:49
  47.4 27.0 %all-to-all-done.1 = f32[128,1,64,128]{3,2,1,0:T(8,128)} async-done(((f32[128,1,64,128]{3,2,1,0:T(8,128)}), f32[128,1,64,128]{3,2,1,0:T(8,128)}, u32[]{:S(2)}, u32[]{:S(2)}) %all-to-all-start.1) | async-done | bytes 4194336 | tf_op jit(solution)/shard_map/all_to_all | solution.py:66
  74.5 9.0 %all-to-all-start = ((f32[512,64,128]{2,1,0:T(8,128)}), f32[512,64,128]{2,1,0:T(8,128)}, u32[]{:S(2)}, u32[]{:S(2)}) async-start(f32[512,64,128]{2,1,0:T(8,128)} %bitcast.59), calls=%async_computation | async-start | bytes 33554432 | tf_op jit(solution)/shard_map/all_to_all | solution.py:56
  83.5 0.1 reshape.204
  83.6 0.1 broadcast_in_dim.108
  83.7 0.1 broadcast_in_dim.109
  83.9 0.1 copy.20
  84.0 0.1 reshape.196
  84.1 0.1 copy.18
  84.2 0.1 broadcast_in_dim.95
  84.3 0.1 broadcast_in_dim.96
  84.5 0.2 clamp_reduce_fusion
  84.7 0.2 and_reduce_fusion
  84.9 2.7 gather_fusion.4
  87.7 0.1 select_select_fusion
  87.7 1.1 convolution_bitcast_fusion.2
  88.8 1.4 convolution_bitcast_fusion.1
  90.2 235.2 %all-to-all-done = f32[512,64,128]{2,1,0:T(8,128)} async-done(((f32[512,64,128]{2,1,0:T(8,128)}), f32[512,64,128]{2,1,0:T(8,128)}, u32[]{:S(2)}, u32[]{:S(2)}) %all-to-all-start) | async-done | bytes 16777248 | tf_op jit(solution)/shard_map/all_to_all | solution.py:56
  325.4 10.1 %gather_fusion.3 = f32[256,64,128]{2,1,0:T(8,128)} fusion(f32[512,64,128]{2,1,0:T(8,128)} %all-to-all-done, s32[1024]{0:T(1024)S(1)} %pad_clamp_fusion.1), kind=kCustom, calls=%fused_computation.3 | custom fusion | bytes 16778240 | tf_op jit(solution)/shard_map/jit(_take)/gather | solution.py:10
  335.5 7.5 %bitcast_select_fusion.1 = f32[8,2048,128]{2,1,0:T(8,128)S(1)} fusion(pred[8,2048]{1,0:T(8,128)(4,1)S(1)} %broadcast_in_dim.109, f32[8,2048,128]{2,1,0:T(8,128)} %bitcast.63), kind=kLoop, calls=%fused_computation.7 | loop fusion | flops 2097152 | bytes 16793600 | tf_op jit(solution)/shard_map/jit(_take)/select_n | solution.py:10
  343.0 0.0 copy-start.1
  343.0 14.3 %fusion.3 = f32[8,64,128]{1,2,0:T(8,128)} fusion(f32[8,64,128]{1,2,0:T(8,128)S(1)} %copy-done.5, f32[8,2048,128]{2,1,0:T(8,128)S(1)} %bitcast_select_fusion.1, f32[8,64,2048]{2,1,0:T(8,128)S(1)} %copy-done.3), kind=kOutput, calls=%fused_computation.16 | convolution fusion | flops 1610678272 | bytes 13107200 | tf_op jit(solution)/shard_map/nkq,nqp->nkp/dot_general | solution.py:12
  357.3 1.2 copy.26
  358.5 0.6 fusion.23
  359.2 3.3 fusion.6
  362.5 11.7 %gather_fusion.2 = f32[384,64,128]{2,1,0:T(8,128)} fusion(f32[512,64,128]{2,1,0:T(8,128)} %all-to-all-done, s32[1024]{0:T(1024)S(1)} %pad_clamp_fusion.2), kind=kCustom, calls=%fused_computation.2 | custom fusion | bytes 25167360 | tf_op jit(solution)/shard_map/jit(_take)/gather | solution.py:10
  374.2 6.1 %bitcast_select_fusion = f32[32,768,128]{2,1,0:T(8,128)S(1)} fusion(pred[32,768]{1,0:T(8,128)(4,1)S(1)} %broadcast_in_dim.96, f32[32,768,128]{2,1,0:T(8,128)} %bitcast.60), kind=kLoop, calls=%fused_computation.6 | loop fusion | flops 3145728 | bytes 25190400 | tf_op jit(solution)/shard_map/jit(_take)/select_n | solution.py:10
  380.3 10.9 %convolution_add_fusion = f32[32,128,64]{1,2,0:T(8,128)S(1)} fusion(f32[32,128,64]{1,2,0:T(8,128)S(1)} %copy-done.2, f32[32,768,128]{2,1,0:T(8,128)S(1)} %bitcast_select_fusion, f32[32,64,768]{2,1,0:T(8,128)} %param.22), kind=kOutput, calls=%fused_computation.14 | convolution fusion | flops 2416181248 | bytes 20971520 | tf_op jit(solution)/shard_map/nkq,nqp->nkp/dot_general | solution.py:12
  391.2 5.2 %multiply_bitcast_fusion = f32[32,256,128]{1,2,0:T(8,128)} fusion(f32[32,128,64]{1,2,0:T(8,128)S(1)} %convolution_add_fusion, f32[32,64,256]{2,1,0:T(8,128)S(1)} %copy-done, f32[32,256]{1,0:T(8,128)S(1)} %fusion.11), kind=kOutput, calls=%fused_computation.8 | convolution fusion | flops 806354944 | bytes 7372800 | tf_op jit(solution)/shard_map/lkm,lkp->lmp/dot_general | solution.py:92
  396.5 5.6 %copy.22 = f32[32,256,128]{2,1,0:T(8,128)} copy(f32[32,256,128]{1,2,0:T(8,128)} %multiply_bitcast_fusion) | data formatting | bytes 8388608 | tf_op jit(solution)/shard_map/mul | solution.py:92
  (34 shorter events, 0.1 us)
Async XLA Ops:
  0.0 2.0 copy-start
  0.0 9.5 %copy-start.10 = (s32[32]{0:T(128)S(1)}, s32[32]{0:T(128)}, u32[]{:S(2)}) copy-start(s32[32]{0:T(128)} %param.19) | copy-start | bytes 388
  7.1 18.6 %copy-start.11 = (s32[256]{0:T(256)S(1)}, s32[256]{0:T(256)}, u32[]{:S(2)}) copy-start(s32[256]{0:T(256)} %param.23) | copy-start | bytes 3076
  7.1 18.7 %copy-start.12 = (s32[256]{0:T(256)S(1)}, s32[256]{0:T(256)}, u32[]{:S(2)}) copy-start(s32[256]{0:T(256)} %param.20) | copy-start | bytes 3076
  10.5 0.7 copy-start.4
  14.4 60.1 %all-to-all-start.1 = ((f32[128,1,64,128]{3,2,1,0:T(8,128)}), f32[128,1,64,128]{3,2,1,0:T(8,128)}, u32[]{:S(2)}, u32[]{:S(2)}) async-start(f32[128,1,64,128]{3,2,1,0:T(8,128)} %stack.3), calls=%async_computation.1 | async-start | bytes 8388608 | tf_op jit(solution)/shard_map/all_to_all | solution.py:66
  74.5 9.1 %copy-start.9 = (s32[8,32]{1,0:T(8,128)S(1)}, s32[8,32]{1,0:T(8,128)}, u32[]{:S(2)}) copy-start(s32[8,32]{1,0:T(8,128)} %param.24) | copy-start | bytes 3076
  74.5 9.4 %copy-start.8 = (s32[32,12]{0,1:T(8,128)S(1)}, s32[32,12]{0,1:T(8,128)}, u32[]{:S(2)}) copy-start(s32[32,12]{0,1:T(8,128)} %param.21) | copy-start | bytes 4612
  74.5 10.0 %copy-start.7 = (s32[32,4]{0,1:T(4,128)S(1)}, s32[32,4]{0,1:T(4,128)}, u32[]{:S(2)}) copy-start(s32[32,4]{0,1:T(4,128)} %param.26) | copy-start | bytes 1540
  74.5 14.3 %copy-start.6 = (f32[8,64,64]{2,1,0:T(8,128)S(1)}, f32[8,64,64]{2,1,0:T(8,128)}, u32[]{:S(2)}) copy-start(f32[8,64,64]{2,1,0:T(8,128)} %param.18) | copy-start | bytes 393220
  74.5 250.9 %all-to-all-start = ((f32[512,64,128]{2,1,0:T(8,128)}), f32[512,64,128]{2,1,0:T(8,128)}, u32[]{:S(2)}, u32[]{:S(2)}) async-start(f32[512,64,128]{2,1,0:T(8,128)} %bitcast.59), calls=%async_computation | async-start | bytes 33554432 | tf_op jit(solution)/shard_map/all_to_all | solution.py:56
  335.5 7.5 %copy-start.3 = (f32[8,64,2048]{2,1,0:T(8,128)S(1)}, f32[8,64,2048]{2,1,0:T(8,128)}, u32[]{:S(2)}) copy-start(f32[8,64,2048]{2,1,0:T(8,128)} %param.25) | copy-start | bytes 12582916
  335.5 7.5 %copy-start.5 = (f32[8,64,128]{1,2,0:T(8,128)S(1)}, f32[8,64,128]{1,2,0:T(8,128)}, u32[]{:S(2)}) copy-start(f32[8,64,128]{1,2,0:T(8,128)} %convolution_bitcast_fusion.1) | copy-start | bytes 786436
  343.0 16.2 %copy-start.1 = (f32[32,64,64]{2,1,0:T(8,128)S(1)}, f32[32,64,64]{2,1,0:T(8,128)}, u32[]{:S(2)}) copy-start(f32[32,64,64]{2,1,0:T(8,128)} %param.17) | copy-start | bytes 1572868
  374.2 6.1 %copy-start.2 = (f32[32,128,64]{1,2,0:T(8,128)S(1)}, f32[32,128,64]{1,2,0:T(8,128)}, u32[]{:S(2)}) copy-start(f32[32,128,64]{1,2,0:T(8,128)} %fusion.6) | copy-start | bytes 3145732
